TPU v7x, 128 devices: a whole 4x4x4 slice. The times are simulated.
128 devices in a mesh: grp: 2 (over y_lo), sp: 64 (over x, y_hi, z, core).
Axes of the slice: x: 4, y: 4 (y_hi: 2, y_lo: 2; y = y_hi * 2 + y_lo), z: 4, core: 2. Of those that a mesh axis runs over, the one named last changes fastest.
Arguments:
- modes: bfloat16 [3, 512, 32, 16, 256], P(None, 'sp', 'grp'), may hold values from -16 to 16
- convecting: int32 [12], replicated, may hold values from 0 to 255, as said below
Outputs:
- skew_tensor: float32 [12, 256, 256], P(None, 'sp')
Inputs may be any that keep to these rules, and one draw needn't show every extreme that they name: `convecting`: 12 distinct mode indices.
All inputs are finite; a program needn't handle non-finite values.
Results may differ from a plain program's by a relative error of at most 0.0029.
Values may be sent and summed in bfloat16 or wider, within the bound.
No kernel may reach another device: no remote copies, remote signals or barrier semaphores. Data moves between devices by JAX's collectives and lax.ppermute only.
A program may use at most 64 MiB of HBM per device.

v0:
```python
import math
import jax
import jax.numpy as jnp
from jax import lax
from jax.sharding import PartitionSpec as P


def extended(block, sides, width):
    for axis, dim in sides:
        count = lax.axis_size(axis)
        forward = [(i, i + 1) for i in range(count - 1)]
        forward.append((count - 1, 0))
        backward = [(target, source) for source, target in forward]
        low = lax.ppermute(
            lax.slice_in_dim(block, block.shape[dim] - width, None, axis=dim), axis, forward
        )
        high = lax.ppermute(lax.slice_in_dim(block, 0, width, axis=dim), axis, backward)
        block = jnp.concatenate([low, block, high], axis=dim)
    return block


def shards(modes, convecting):
    n_sp = lax.axis_size("sp")
    n_grp = lax.axis_size("grp")
    width = modes.shape[4]
    cells = modes.shape[1] * n_sp * modes.shape[2] * n_grp * modes.shape[3]
    padded = extended(modes, (("grp", 2), ("sp", 1)), 1)
    picker = (jnp.arange(width, dtype=jnp.int32)[:, None] == convecting[None, :]).astype(
        jnp.bfloat16
    )
    velocity = jnp.einsum("cxyzm,ms->scxyz", modes, picker, preferred_element_type=jnp.float32)
    test_flat = modes.reshape(-1, width)

    def project(carry, field):
        centre = padded[:, 1:-1, 1:-1].astype(jnp.float32)
        along_x = padded[:, 2:, 1:-1].astype(jnp.float32) - padded[:, :-2, 1:-1].astype(jnp.float32)
        along_y = padded[:, 1:-1, 2:].astype(jnp.float32) - padded[:, 1:-1, :-2].astype(jnp.float32)
        along_z = jnp.roll(centre, -1, axis=3) - jnp.roll(centre, 1, axis=3)
        moved = 0.5 * (
            field[0][..., None] * along_x
            + field[1][..., None] * along_y
            + field[2][..., None] * along_z
        )
        moved = moved.astype(jnp.bfloat16).reshape(-1, width)
        block = lax.dot_general(
            test_flat, moved, (((0,), (0,)), ((), ())), preferred_element_type=jnp.float32
        )
        return (carry, block)

    _, stacked = lax.scan(project, jnp.zeros((), jnp.float32), velocity)
    mine = lax.psum_scatter(stacked, "sp", scatter_dimension=1, tiled=True)
    owned = lax.psum(mine, "grp")
    owned = owned / math.sqrt(cells)
    mirrored = lax.all_to_all(owned, "sp", split_axis=2, concat_axis=1, tiled=True)
    return 0.5 * (owned - jnp.swapaxes(mirrored, 1, 2))


def solution(mesh):
    placed = (P(None, "sp", "grp", None, None), P())
    return jax.shard_map(
        shards, mesh=mesh, in_specs=placed, out_specs=P(None, "sp", None), check_vma=False
    )
```

profile of v0, /device:TPU:1, one launch (start us, length us, event | category | flops | bytes accessed | tf_op | source)
XLA Modules:
  0.0 910.7 jit_solution(5108024089505814859)
XLA Ops:
  7.6 2.2 collective-permute-start
  9.9 4.2 collective-permute-done
  14.1 2.3 constant_dynamic-update-slice_fusion.2
  16.4 1.8 collective-permute-done.1
  18.3 1.7 copy-done.1
  21.0 3.3 collective-permute-start.2
  24.3 5.6 fusion.6
  29.9 2.7 collective-permute-done.3
  32.7 3.4 pad_maximum_fusion
  36.1 183.5 %while.10 = (s32[]{:T(128)}, f32[12,256,256]{2,1,0:T(8,128)}, f32[12,3,8,16,16]{4,0,3,2,1:T(8,128)}, bf16[3,10,18,16,256]{4,3,2,1,0:T(8,128)(2,1)}, bf16[3,8,18,...) while((s32[]{:T(128)}, f32[12,256,256]{2,1,0:T(8,128)}, ...), condition=%wide.region_1.2_spmd, body=%wide.region_0.1_spmd.sunk | while | flops 830472192 | bytes 61203032 | solution.py:50
  37.6 1.9 fusion.24
  40.4 7.4 fusion.25
  47.8 1.7 convolution_bitcast_fusion.2
  52.9 1.9 fusion.24
  55.7 7.4 fusion.25
  63.1 1.7 convolution_bitcast_fusion.2
  68.2 1.9 fusion.24
  71.0 7.4 fusion.25
  78.4 1.7 convolution_bitcast_fusion.2
  83.5 1.9 fusion.24
  86.3 7.4 fusion.25
  93.7 1.7 convolution_bitcast_fusion.2
  98.8 1.9 fusion.24
  101.6 7.4 fusion.25
  109.0 1.7 convolution_bitcast_fusion.2
  114.1 1.9 fusion.24
  116.9 7.4 fusion.25
  124.3 1.7 convolution_bitcast_fusion.2
  129.4 1.9 fusion.24
  132.2 7.4 fusion.25
  139.6 1.7 convolution_bitcast_fusion.2
  144.7 1.9 fusion.24
  147.5 7.4 fusion.25
  160.0 1.9 fusion.24
  162.8 7.4 fusion.25
  170.2 1.7 convolution_bitcast_fusion.2
  175.3 1.9 fusion.24
  178.1 7.4 fusion.25
  185.5 1.7 convolution_bitcast_fusion.2
  190.6 1.9 fusion.24
  193.3 7.4 fusion.25
  200.7 1.7 convolution_bitcast_fusion.2
  205.8 1.9 fusion.24
  208.6 7.4 fusion.25
  216.0 1.7 convolution_bitcast_fusion.2
  220.8 651.3 %all-reduce.3.cloned.1.call-done = f32[12,256,256]{2,1,0:T(8,128)} async-done(((f32[12,256,256]{2,1,0:T(8,128)}), f32[12,256,256]{2,1,0:T(8,128)}) %all-reduce.3.cloned.1.call-update) | async-done | bytes 3145744
  873.0 5.7 psum.7
  879.6 21.0 %all_to_all.18 = f32[64,1,192]{2,1,0:T(1,128)S(1)} all-to-all(f32[64,1,192]{2,1,0:T(1,128)S(1)} %reshape.21), channel_id=1, replica_groups=mesh['grp'=2,'sp'=64] {'sp'}, dimensions={0} | all-to-all | bytes 98304 | tf_op jit(solution)/shard_map/all_to_all | solution.py:54
  (92 shorter events, 60.0 us)
Async XLA Ops:
  6.5 865.5 %all-reduce.3.cloned.1.call-start = ((), (), s32[]{:S(2)}) async-start(), calls=%async_computation.1 | async-start | bytes 6291456
  7.6 6.5 collective-permute-start
  9.8 8.5 collective-permute-start.1
  14.1 10.2 %copy-start = (bf16[3,8,16,16,256]{4,3,2,1,0:T(8,128)(2,1)S(1)}, bf16[3,8,16,16,256]{4,3,2,1,0:T(8,128)(2,1)}, u32[]{:S(2)}) copy-start(bf16[3,8,16,16,256]{4,3,2,1,0:T(8,128)(2,1)} %param.4) | copy-start | bytes 9437188
  14.1 10.2 %copy-start.3 = (s32[12]{0:T(128)S(1)}, s32[12]{0:T(128)}, u32[]{:S(2)}) copy-start(s32[12]{0:T(128)} %param.5) | copy-start | bytes 148
  18.3 1.8 copy-start.1
  21.0 8.9 collective-permute-start.2
  24.3 8.3 collective-permute-start.3
  24.3 8.3 copy-start.2
  36.1 183.5 %copy-start.4 = (u32[128]{0:T(128)S(1)}, u32[128]{0:T(128)}, u32[]{:S(2)}) copy-start(u32[128]{0:T(128)} %constant.23) | copy-start | bytes 1540
Sparse Core Ops, SparseCore 0:
  219.7 652.3 all-reduce.2
where the time goes:
time: 912 us; the launch traced here: 911 us
  waiting for transfers between devices  660 us (72%)
  other arithmetic  93.7 us (10%)
  local copies, waits for them, and re-layouts  83.7 us (9%)
  blocking collectives  26.7 us (3%)
  matrix products  26.2 us (3%)
  between operations  14.2 us (2%)
    unnamed x2, waiting for transfers between devices  651 us
    convert_element_type x12, other arithmetic, project(): moved = moved.astype(jnp.bfloat16).reshape(-1, width)  88.8 us
    slice x24, local copies, waits for them, and re-layouts, project(): along_z = jnp.roll(centre, -1, axis=3) - jnp.roll(centre, 1, axis=3)  33.1 us
    dynamic_update_slice x24, local copies, waits for them, and re-layouts, shards(): _, stacked = lax.scan(project, jnp.zeros((), jnp.float32), velocity)  21.6 us
    all_to_all x1, blocking collectives, shards(): lax.all_to_all(owned, 'sp', split_axis=2, concat_axis=1, tiled=True)  21 us
    dot_general x12, matrix products, project(): lax.dot_general(test_flat, moved, (((0,), (0,)), ((), ())), preferred_ele...  20.6 us
    dynamic_slice x12, local copies, waits for them, and re-layouts, shards(): _, stacked = lax.scan(project, jnp.zeros((), jnp.float32), velocity)  18.6 us
  transfers between devices with their start and end apart: 5, of which 4 were waited for; matrix products, arithmetic and copies ran while one was open for 1% of the time, Pallas kernels for 0%

commit v1 on v0

--- a/solution.py
+++ b/solution.py
@@ -51,7 +51,9 @@
     mine = lax.psum_scatter(stacked, "sp", scatter_dimension=1, tiled=True)
     owned = lax.psum(mine, "grp")
     owned = owned / math.sqrt(cells)
-    mirrored = lax.all_to_all(owned, "sp", split_axis=2, concat_axis=1, tiled=True)
+    mirrored = jnp.concatenate(
+        lax.all_to_all(jnp.stack(jnp.split(owned, lax.axis_size("sp"), axis=2)), "sp", 0, 0), axis=1
+    )
     return 0.5 * (owned - jnp.swapaxes(mirrored, 1, 2))
 
 

time: 912 us -> 653 us (0.72)
  waiting for transfers between devices: 660 us -> 397 us
  blocking collectives: 26.7 us -> 36.5 us
    unnamed x2 -> x1, waiting for transfers between devices: 651 us -> 0.02 us
    reduce_scatter x0 -> x1, waiting for transfers between devices: none -> 388 us  [shards(): mine = lax.psum_scatter(stacked, 'sp', scatter_dimension=1, tiled=True)]
    dynamic_update_slice x24 -> x0, local copies, waits for them, and re-layouts: 21.6 us -> none  [shards(): _, stacked = lax.scan(project, jnp.zeros((), jnp.float32), velocity)]
    while x0 -> x1, local copies, waits for them, and re-layouts: none -> 17.9 us  [shards(): _, stacked = lax.scan(project, jnp.zeros((), jnp.float32), velocity)]
where the time goes in v1:
time: 653 us; the launch traced here: 652 us
  waiting for transfers between devices  397 us (61%)
  other arithmetic  93.1 us (14%)
  local copies, waits for them, and re-layouts  79.4 us (12%)
  blocking collectives  36.5 us (6%)
  matrix products  26.2 us (4%)
  between operations  13.8 us (2%)
    reduce_scatter x1, waiting for transfers between devices, shards(): mine = lax.psum_scatter(stacked, 'sp', scatter_dimension=1, tiled=True)  388 us
    convert_element_type x12, other arithmetic, project(): moved = moved.astype(jnp.bfloat16).reshape(-1, width)  88.8 us
    slice x24, local copies, waits for them, and re-layouts, project(): along_z = jnp.roll(centre, -1, axis=3) - jnp.roll(centre, 1, axis=3)  33.1 us
    all_to_all x1, blocking collectives, shards(): lax.all_to_all(jnp.stack(jnp.split(owned, lax.axis_size('sp'), axis=2)),...  23.9 us
    dot_general x12, matrix products, project(): lax.dot_general(test_flat, moved, (((0,), (0,)), ((), ())), preferred_ele...  20.6 us
    dynamic_slice x12, local copies, waits for them, and re-layouts, shards(): _, stacked = lax.scan(project, jnp.zeros((), jnp.float32), velocity)  18.6 us
    while x1, local copies, waits for them, and re-layouts, shards(): _, stacked = lax.scan(project, jnp.zeros((), jnp.float32), velocity)  17.9 us
  transfers between devices with their start and end apart: 5, of which 4 were waited for; matrix products, arithmetic and copies ran while one was open for 1% of the time, Pallas kernels for 0%

profile of v1, /device:TPU:1, one launch (start us, length us, event | category | flops | bytes accessed | tf_op | source)
XLA Modules:
  0.0 652.1 jit_solution(13791874989647685911)
XLA Ops:
  7.6 2.2 collective-permute-start
  9.9 4.2 collective-permute-done
  14.1 2.3 constant_dynamic-update-slice_fusion.1
  16.4 1.8 collective-permute-done.1
  18.3 1.8 copy-done.1
  21.1 3.3 collective-permute-start.2
  24.4 5.6 fusion.6
  30.0 2.7 collective-permute-done.3
  32.7 3.4 pad_maximum_fusion
  36.0 161.7 %while.10 = (s32[]{:T(128)}, f32[12,256,256]{1,2,0:T(8,128)}, f32[12,3,8,16,16]{4,0,3,2,1:T(8,128)}, bf16[3,10,18,16,256]{4,3,2,1,0:T(8,128)(2,1)}, bf16[3,8,18,...) while((s32[]{:T(128)}, f32[12,256,256]{1,2,0:T(8,128)}, ...), condition=%wide.region_1.2_spmd, body=%wide.region_0.1_spmd.sunk | while | flops 830472192 | bytes 60154456 | solution.py:50
  37.6 1.9 fusion.25
  40.4 7.4 %fusion.26 = bf16[3,8,16,16,256]{4,3,2,1,0:T(8,128)(2,1)S(1)} fusion(f32[3,8,16,1,256]{4,3,2,1,0:T(1,128)S(1)} %get-tuple-element.160, f32[3,8,16,15,256]{4,3,2,1,0:T(8,128)S(1)} %get-tuple-element.161, f32[3,8,16,15,256]{4,3,2,1,0:T(8,128)S(1)} %get-tuple-element.162, f32[3,8,16,1,256]{4,3,2,1,0:T(1,128)S(1)} %get-tuple-element.163, ...), kind=kLoop, calls=%fused_computation.4.clone.1 | loop fusion | flops 25165824 | bytes 28336128 | tf_op jit(solution)/shard_map/while/body/eval_jaxpr/convert_element_type | solution.py:44
  47.8 1.7 fusion.27
  51.1 1.9 fusion.25
  53.9 7.4 %fusion.26 = bf16[3,8,16,16,256]{4,3,2,1,0:T(8,128)(2,1)S(1)} fusion(f32[3,8,16,1,256]{4,3,2,1,0:T(1,128)S(1)} %get-tuple-element.160, f32[3,8,16,15,256]{4,3,2,1,0:T(8,128)S(1)} %get-tuple-element.161, f32[3,8,16,15,256]{4,3,2,1,0:T(8,128)S(1)} %get-tuple-element.162, f32[3,8,16,1,256]{4,3,2,1,0:T(1,128)S(1)} %get-tuple-element.163, ...), kind=kLoop, calls=%fused_computation.4.clone.1 | loop fusion | flops 25165824 | bytes 28336128 | tf_op jit(solution)/shard_map/while/body/eval_jaxpr/convert_element_type | solution.py:44
  61.3 1.7 fusion.27
  64.6 1.9 fusion.25
  67.3 7.4 %fusion.26 = bf16[3,8,16,16,256]{4,3,2,1,0:T(8,128)(2,1)S(1)} fusion(f32[3,8,16,1,256]{4,3,2,1,0:T(1,128)S(1)} %get-tuple-element.160, f32[3,8,16,15,256]{4,3,2,1,0:T(8,128)S(1)} %get-tuple-element.161, f32[3,8,16,15,256]{4,3,2,1,0:T(8,128)S(1)} %get-tuple-element.162, f32[3,8,16,1,256]{4,3,2,1,0:T(1,128)S(1)} %get-tuple-element.163, ...), kind=kLoop, calls=%fused_computation.4.clone.1 | loop fusion | flops 25165824 | bytes 28336128 | tf_op jit(solution)/shard_map/while/body/eval_jaxpr/convert_element_type | solution.py:44
  74.7 1.7 fusion.27
  78.0 1.9 fusion.25
  80.8 7.4 %fusion.26 = bf16[3,8,16,16,256]{4,3,2,1,0:T(8,128)(2,1)S(1)} fusion(f32[3,8,16,1,256]{4,3,2,1,0:T(1,128)S(1)} %get-tuple-element.160, f32[3,8,16,15,256]{4,3,2,1,0:T(8,128)S(1)} %get-tuple-element.161, f32[3,8,16,15,256]{4,3,2,1,0:T(8,128)S(1)} %get-tuple-element.162, f32[3,8,16,1,256]{4,3,2,1,0:T(1,128)S(1)} %get-tuple-element.163, ...), kind=kLoop, calls=%fused_computation.4.clone.1 | loop fusion | flops 25165824 | bytes 28336128 | tf_op jit(solution)/shard_map/while/body/eval_jaxpr/convert_element_type | solution.py:44
  88.2 1.7 fusion.27
  91.5 1.9 fusion.25
  94.3 7.4 %fusion.26 = bf16[3,8,16,16,256]{4,3,2,1,0:T(8,128)(2,1)S(1)} fusion(f32[3,8,16,1,256]{4,3,2,1,0:T(1,128)S(1)} %get-tuple-element.160, f32[3,8,16,15,256]{4,3,2,1,0:T(8,128)S(1)} %get-tuple-element.161, f32[3,8,16,15,256]{4,3,2,1,0:T(8,128)S(1)} %get-tuple-element.162, f32[3,8,16,1,256]{4,3,2,1,0:T(1,128)S(1)} %get-tuple-element.163, ...), kind=kLoop, calls=%fused_computation.4.clone.1 | loop fusion | flops 25165824 | bytes 28336128 | tf_op jit(solution)/shard_map/while/body/eval_jaxpr/convert_element_type | solution.py:44
  101.7 1.7 fusion.27
  105.0 1.9 fusion.25
  107.8 7.4 %fusion.26 = bf16[3,8,16,16,256]{4,3,2,1,0:T(8,128)(2,1)S(1)} fusion(f32[3,8,16,1,256]{4,3,2,1,0:T(1,128)S(1)} %get-tuple-element.160, f32[3,8,16,15,256]{4,3,2,1,0:T(8,128)S(1)} %get-tuple-element.161, f32[3,8,16,15,256]{4,3,2,1,0:T(8,128)S(1)} %get-tuple-element.162, f32[3,8,16,1,256]{4,3,2,1,0:T(1,128)S(1)} %get-tuple-element.163, ...), kind=kLoop, calls=%fused_computation.4.clone.1 | loop fusion | flops 25165824 | bytes 28336128 | tf_op jit(solution)/shard_map/while/body/eval_jaxpr/convert_element_type | solution.py:44
  115.2 1.7 fusion.27
  118.5 1.9 fusion.25
  121.3 7.4 %fusion.26 = bf16[3,8,16,16,256]{4,3,2,1,0:T(8,128)(2,1)S(1)} fusion(f32[3,8,16,1,256]{4,3,2,1,0:T(1,128)S(1)} %get-tuple-element.160, f32[3,8,16,15,256]{4,3,2,1,0:T(8,128)S(1)} %get-tuple-element.161, f32[3,8,16,15,256]{4,3,2,1,0:T(8,128)S(1)} %get-tuple-element.162, f32[3,8,16,1,256]{4,3,2,1,0:T(1,128)S(1)} %get-tuple-element.163, ...), kind=kLoop, calls=%fused_computation.4.clone.1 | loop fusion | flops 25165824 | bytes 28336128 | tf_op jit(solution)/shard_map/while/body/eval_jaxpr/convert_element_type | solution.py:44
  128.7 1.7 fusion.27
  132.0 1.9 fusion.25
  134.7 7.4 %fusion.26 = bf16[3,8,16,16,256]{4,3,2,1,0:T(8,128)(2,1)S(1)} fusion(f32[3,8,16,1,256]{4,3,2,1,0:T(1,128)S(1)} %get-tuple-element.160, f32[3,8,16,15,256]{4,3,2,1,0:T(8,128)S(1)} %get-tuple-element.161, f32[3,8,16,15,256]{4,3,2,1,0:T(8,128)S(1)} %get-tuple-element.162, f32[3,8,16,1,256]{4,3,2,1,0:T(1,128)S(1)} %get-tuple-element.163, ...), kind=kLoop, calls=%fused_computation.4.clone.1 | loop fusion | flops 25165824 | bytes 28336128 | tf_op jit(solution)/shard_map/while/body/eval_jaxpr/convert_element_type | solution.py:44
  142.1 1.7 fusion.27
  145.4 1.9 fusion.25
  148.2 7.4 %fusion.26 = bf16[3,8,16,16,256]{4,3,2,1,0:T(8,128)(2,1)S(1)} fusion(f32[3,8,16,1,256]{4,3,2,1,0:T(1,128)S(1)} %get-tuple-element.160, f32[3,8,16,15,256]{4,3,2,1,0:T(8,128)S(1)} %get-tuple-element.161, f32[3,8,16,15,256]{4,3,2,1,0:T(8,128)S(1)} %get-tuple-element.162, f32[3,8,16,1,256]{4,3,2,1,0:T(1,128)S(1)} %get-tuple-element.163, ...), kind=kLoop, calls=%fused_computation.4.clone.1 | loop fusion | flops 25165824 | bytes 28336128 | tf_op jit(solution)/shard_map/while/body/eval_jaxpr/convert_element_type | solution.py:44
  155.6 1.7 fusion.27
  158.9 1.9 fusion.25
  161.7 7.4 %fusion.26 = bf16[3,8,16,16,256]{4,3,2,1,0:T(8,128)(2,1)S(1)} fusion(f32[3,8,16,1,256]{4,3,2,1,0:T(1,128)S(1)} %get-tuple-element.160, f32[3,8,16,15,256]{4,3,2,1,0:T(8,128)S(1)} %get-tuple-element.161, f32[3,8,16,15,256]{4,3,2,1,0:T(8,128)S(1)} %get-tuple-element.162, f32[3,8,16,1,256]{4,3,2,1,0:T(1,128)S(1)} %get-tuple-element.163, ...), kind=kLoop, calls=%fused_computation.4.clone.1 | loop fusion | flops 25165824 | bytes 28336128 | tf_op jit(solution)/shard_map/while/body/eval_jaxpr/convert_element_type | solution.py:44
  169.1 1.7 fusion.27
  172.4 1.9 fusion.25
  175.2 7.4 %fusion.26 = bf16[3,8,16,16,256]{4,3,2,1,0:T(8,128)(2,1)S(1)} fusion(f32[3,8,16,1,256]{4,3,2,1,0:T(1,128)S(1)} %get-tuple-element.160, f32[3,8,16,15,256]{4,3,2,1,0:T(8,128)S(1)} %get-tuple-element.161, f32[3,8,16,15,256]{4,3,2,1,0:T(8,128)S(1)} %get-tuple-element.162, f32[3,8,16,1,256]{4,3,2,1,0:T(1,128)S(1)} %get-tuple-element.163, ...), kind=kLoop, calls=%fused_computation.4.clone.1 | loop fusion | flops 25165824 | bytes 28336128 | tf_op jit(solution)/shard_map/while/body/eval_jaxpr/convert_element_type | solution.py:44
  185.9 1.9 fusion.25
  188.7 7.4 %fusion.26 = bf16[3,8,16,16,256]{4,3,2,1,0:T(8,128)(2,1)S(1)} fusion(f32[3,8,16,1,256]{4,3,2,1,0:T(1,128)S(1)} %get-tuple-element.160, f32[3,8,16,15,256]{4,3,2,1,0:T(8,128)S(1)} %get-tuple-element.161, f32[3,8,16,15,256]{4,3,2,1,0:T(8,128)S(1)} %get-tuple-element.162, f32[3,8,16,1,256]{4,3,2,1,0:T(1,128)S(1)} %get-tuple-element.163, ...), kind=kLoop, calls=%fused_computation.4.clone.1 | loop fusion | flops 25165824 | bytes 28336128 | tf_op jit(solution)/shard_map/while/body/eval_jaxpr/convert_element_type | solution.py:44
  197.8 17.9 %copy.217 = f32[12,256,256]{0,2,1:T(8,128)} copy(f32[12,256,256]{1,2,0:T(8,128)} %get-tuple-element.42) | data formatting | bytes 6291456 | tf_op jit(solution)/shard_map/while | solution.py:50
  215.7 388.3 %reduce-scatter.2.cloned.1.call-done = f32[12,4,256]{0,2,1:T(8,128)} async-done(((f32[12,256,256]{0,2,1:T(8,128)}), f32[12,4,256]{0,2,1:T(8,128)}) %reduce-scatter.2.cloned.1.call-update) | async-done | bytes 49168 | tf_op jit(solution)/shard_map/reduce_scatter | solution.py:51
  603.9 12.6 %psum.7 = f32[12,4,256]{0,2,1:T(8,128)S(1)} all-reduce(f32[12,4,256]{0,2,1:T(8,128)} %reduce-scatter.2.cloned.1.call-done), channel_id=1, replica_groups=mesh['grp'=2,'sp'=64] {'grp'}, use_global_device_ids=true, to_apply=%region_3.4 | all-reduce | flops 12288 | bytes 98304 | tf_op jit(solution)/shard_map/psum | solution.py:52
  618.3 23.9 %all_to_all.5 = f32[64,1,192]{2,1,0:T(1,128)S(1)} all-to-all(f32[64,1,192]{2,1,0:T(1,128)S(1)} %reshape.26), channel_id=1, replica_groups=mesh['grp'=2,'sp'=64] {'sp'}, dimensions={0} | all-to-all | bytes 98304 | tf_op jit(solution)/shard_map/all_to_all | solution.py:55
  (128 shorter events, 39.0 us)
Async XLA Ops:
  6.5 597.4 %reduce-scatter.2.cloned.1.call-start = ((), (), s32[]{:S(2)}) async-start(), calls=%async_computation.2 | async-start | bytes 34078720 | tf_op jit(solution)/shard_map/reduce_scatter | solution.py:51
  7.6 6.5 collective-permute-start
  9.8 8.5 %collective-permute-start.1 = (bf16[3,8,1,16,256]{4,3,2,1,0:T(8,128)(2,1)S(1)}, bf16[3,8,1,16,256]{4,3,2,1,0:T(8,128)(2,1)S(1)}, u32[]{:S(2)}, u32[]{:S(2)}) collective-permute-start(bf16[3,8,1,16,256]{4,3,2,1,0:T(8,128)(2,1)S(1)} %get-tuple-element.108), channel_id=1, source_target_pairs={{64,0},{0,64},{65,1},{1,65},{66,2},{2,66},{67,3},{3,67},{68,4},{4,... | collective-permute-start | bytes 589832 | tf_op jit(solution)/shard_map/ppermute | solution.py:17
  14.1 10.3 %copy-start = (bf16[3,8,16,16,256]{4,3,2,1,0:T(8,128)(2,1)S(1)}, bf16[3,8,16,16,256]{4,3,2,1,0:T(8,128)(2,1)}, u32[]{:S(2)}) copy-start(bf16[3,8,16,16,256]{4,3,2,1,0:T(8,128)(2,1)} %param.4) | copy-start | bytes 9437188
  14.1 10.2 %copy-start.3 = (s32[12]{0:T(128)S(1)}, s32[12]{0:T(128)}, u32[]{:S(2)}) copy-start(s32[12]{0:T(128)} %param.5) | copy-start | bytes 148
  18.3 1.8 copy-start.1
  21.1 8.9 %collective-permute-start.2 = (bf16[3,1,18,16,256]{4,3,2,1,0:T(8,128)(2,1)}, bf16[3,1,18,16,256]{4,3,2,1,0:T(8,128)(2,1)}, u32[]{:S(2)}, u32[]{:S(2)}) collective-permute-start(bf16[3,1,18,16,256]{4,3,2,1,0:T(8,128)(2,1)} %get-tuple-element.106), channel_id=1, source_target_pairs={{0,1},{1,2},{2,3},{3,4},{4,5},{5,6},{6,7},{7,8},{8,9},{9,10},{10,1... | collective-permute-start | bytes 1327112 | tf_op jit(solution)/shard_map/ppermute | solution.py:14
  24.3 8.3 %collective-permute-start.3 = (bf16[3,1,18,16,256]{4,3,2,1,0:T(8,128)(2,1)}, bf16[3,1,18,16,256]{4,3,2,1,0:T(8,128)(2,1)}, u32[]{:S(2)}, u32[]{:S(2)}) collective-permute-start(bf16[3,1,18,16,256]{4,3,2,1,0:T(8,128)(2,1)} %get-tuple-element.107), channel_id=1, source_target_pairs={{1,0},{2,1},{3,2},{4,3},{5,4},{6,5},{7,6},{8,7},{9,8},{10,9},{11,1... | collective-permute-start | bytes 1327112 | tf_op jit(solution)/shard_map/ppermute | solution.py:17
  24.3 8.3 %copy-start.2 = (bf16[3,8,18,16,256]{4,3,2,1,0:T(8,128)(2,1)S(1)}, bf16[3,8,18,16,256]{4,3,2,1,0:T(8,128)(2,1)}, u32[]{:S(2)}) copy-start(bf16[3,8,18,16,256]{4,3,2,1,0:T(8,128)(2,1)} %copy-done.1) | copy-start | bytes 10616836
Sparse Core Ops, SparseCore 0:
  215.8 388.1 reduce-scatter.1
